TPU v7x, 32 devices: a whole 2x2x4 slice. The times are simulated.
32 devices in a mesh: section: 2 (over core), row: 4 (over y, x), col: 4 (over z).
Axes of the slice: x: 2, y: 2, z: 4, core: 2. Of those that a mesh axis runs over, the one named last changes fastest.
Arguments:
- out_grad: bfloat16 [2048, 256], P(('row', 'col')), may hold values from -6 to 6
- pre_act: bfloat16 [2, 2048, 256], P('section', ('row', 'col')), may hold values from -6 to 6
- aggregated: bfloat16 [2, 2048, 256], P('section', ('row', 'col')), may hold values from -6 to 6
- weights: bfloat16 [2, 256, 256], P('section'), may hold values from -0.375 to 0.375
- tiles: bfloat16 [4, 4, 64, 128, 128], P('row', 'col'), may hold values from -0.109375 to 0.109375
- tile_index: int32 [4, 4, 64, 2], P('row', 'col'), may hold values from 0 to 3, as said below
- live_count: int32 [4, 4], P('row', 'col'), may hold values from 8 to 64, as said below
Outputs:
- weight_grad: float32 [2, 256, 256], P('section')
- feature_grads: bfloat16 [2, 2048, 256], P('section', ('row', 'col'))
Inputs may be any that keep to these rules, and one draw needn't show every extreme that they name: `tile_index`: both entries index blocks of the tile: the first is under 4, the second under 4. `live_count`: some tile uses all 64 slots.
All inputs are finite; a program needn't handle non-finite values.
Results may differ from a plain program's by a relative error of at most 0.012.
Values may be sent and summed in bfloat16 or wider, within the bound.
A program may use at most 64 MiB of HBM per device.

v0:
```python
import math
import jax
import jax.numpy as jnp
from jax import lax
from jax.sharding import PartitionSpec as P


def from_behind(value, axis, steps):
    count = lax.axis_size(axis)
    leading, last = (max(0, -steps), min(count, count - steps))
    return lax.ppermute(value, axis, [(source, source + steps) for source in range(leading, last)])


def on_device(out_grad, pre_act, aggregated, weights, tiles, tile_index, live_count):
    section_id = lax.axis_index("section")
    upper = section_id == 1
    pre_layer = pre_act[0]
    saved_agg = aggregated[0]
    weight_mat = weights[0]
    tile_blocks = tiles[0, 0]
    tile_slots = tile_index[0, 0]
    tile_count = live_count[0, 0]
    node_rows = out_grad.shape[0]
    width = out_grad.shape[1]
    slot_total = tile_blocks.shape[0]
    block = tile_blocks.shape[1]
    tile_rows = node_rows * lax.axis_size("col")
    row_blocks = tile_rows // block
    group = min(32, slot_total)
    groups = slot_total // group
    grouped_slots = tile_slots.reshape(groups, group, 2)
    all_targets = jnp.arange(row_blocks, dtype=jnp.int32)

    def spread(row_grad):
        return lax.all_gather(row_grad, "row", axis=0, tiled=True)

    def block_total(source, col_blocks):
        height = source.shape[1]
        grouped_blocks = source.reshape(groups, group, height, block)

        def group_term(total, blocks_here, slots_here, first_slot):
            picked = jnp.take(col_blocks, slots_here[:, 1], axis=0)
            products = jnp.einsum(
                "sij,sjf->sif", blocks_here, picked, preferred_element_type=jnp.float32
            )
            slot_ids = first_slot + jnp.arange(group, dtype=jnp.int32)
            live = slot_ids < tile_count
            select = ((slots_here[:, 0][None, :] == all_targets[:, None]) & live[None, :]).astype(
                jnp.float32
            )
            return total + jnp.einsum("bs,sif->bif", select, products)

        start_total = jnp.zeros((row_blocks, height, width), jnp.float32)

        def scan_step(total, group_id):
            blocks_here = lax.dynamic_index_in_dim(grouped_blocks, group_id, 0, False)
            slots_here = lax.dynamic_index_in_dim(grouped_slots, group_id, 0, False)
            return (group_term(total, blocks_here, slots_here, group_id * group), None)

        total, _ = lax.scan(scan_step, start_total, jnp.arange(groups, dtype=jnp.int32))
        return total.reshape(row_blocks * height, width)

    def reduce_col(source, gathered):
        col_blocks = gathered.reshape(-1, block, width)
        height = source.shape[1]
        return lax.psum_scatter(
            block_total(source, col_blocks), "col", scatter_dimension=0, tiled=True
        )

    def local_terms(incoming):
        masked = jnp.where(pre_layer > 0, incoming, jnp.zeros_like(incoming))
        weight_term = lax.dot_general(
            saved_agg, masked, (((0,), (0,)), ((), ())), preferred_element_type=jnp.float32
        )
        row_grad = lax.dot_general(
            masked, weight_mat, (((1,), (1,)), ((), ())), preferred_element_type=jnp.float32
        ).astype(jnp.bfloat16)
        return (weight_term, row_grad)

    def backward_step(incoming):
        weight_term, row_grad = local_terms(incoming)
        summed = reduce_col(tile_blocks, spread(row_grad))
        return (weight_term, summed.astype(jnp.bfloat16))

    first_input = jnp.where(upper, out_grad, jnp.zeros_like(out_grad))
    first_weight, first_grad = backward_step(first_input)
    received = from_behind(first_grad, "section", -1)
    second_weight, second_grad = backward_step(received)
    local_weight = jnp.where(upper, first_weight, second_weight)
    feature_block = jnp.where(upper, first_grad, second_grad)
    total_weight = lax.psum(local_weight, ("row", "col"))
    node_total = node_rows * lax.axis_size("row") * lax.axis_size("col")
    weight_grad = (total_weight * (1.0 / math.sqrt(node_total)))[None]
    return (weight_grad, feature_block[None])


def solution(mesh):
    placed = (
        P(("row", "col"), None),
        P("section", ("row", "col"), None),
        P("section", ("row", "col"), None),
        P("section", None, None),
        P("row", "col", None, None, None),
        P("row", "col", None, None),
        P("row", "col"),
    )
    return jax.shard_map(
        on_device,
        mesh=mesh,
        in_specs=placed,
        out_specs=(P("section", None, None), P("section", ("row", "col"), None)),
        check_vma=False,
    )
```

profile of v0, /device:TPU:0, one launch (start us, length us, event | category | flops | bytes accessed | tf_op | source)
XLA Modules:
  0.0 212.3 jit_solution(15838875846190478118)
XLA Ops:
  7.2 0.9 broadcast_compare_fusion
  8.3 10.5 %all_gather.6 = bf16[512,256]{1,0:T(8,128)(2,1)S(1)} all-gather(bf16[128,256]{1,0:T(8,128)(2,1)S(1)} %convolution_convert_fusion.1), channel_id=1, replica_groups=mesh['section'=2,'row'=4,'col'=4] {'row'}, dimensions={0}, use_global_device_ids=true | all-gather | bytes 327680 | tf_op jit(solution)/shard_map/all_gather | solution.py:35
  18.8 0.8 reshape_squeeze.7
  19.6 20.1 %while.22 = (s32[]{:T(128)}, f32[4,128,256]{2,0,1:T(4,128)S(1)}, s32[2]{0:T(128)S(1)}, s32[2,32,2]{1,2,0:T(2,128)S(1)}, s32[]{:T(128)}, /*index=5*/bf16[2,32,128...) while((s32[]{:T(128)}, f32[4,128,256]{2,0,1:T(4,128)S(1)}, ...), condition=%wide.region_1.3_spmd.clone, body=%wide.region_0.2_spmd.clone.sunk | while | flops 278136320 | bytes 12588737 | solution.py:60
  22.2 2.0 gather_fusion
  24.2 2.7 %fusion.70 = bf16[32,128,256]{2,1,0:T(8,128)(2,1)S(1)} fusion(bf16[32,128,256]{2,1,0:T(8,128)(2,1)} %gather_fusion, pred[32]{0:T(512)(128)(4,1)S(1)} %get-tuple-element.273, bf16[2,32,128,128]{3,2,1,0:T(8,128)(2,1)} %get-tuple-element.310, s32[]{:T(128)S(6)} %select_n.94), kind=kOutput, calls=%fused_computation.6.clone.1 | convolution fusion | flops 269484032 | bytes 5242916 | tf_op jit(solution)/shard_map/while/body/eval_jaxpr/sij,sjf->sif/dot_general | solution.py:43
  27.6 0.7 add_compare_fusion.4
  28.2 1.4 fusion.71
  32.3 2.0 gather_fusion
  34.3 2.7 %fusion.70 = bf16[32,128,256]{2,1,0:T(8,128)(2,1)S(1)} fusion(bf16[32,128,256]{2,1,0:T(8,128)(2,1)} %gather_fusion, pred[32]{0:T(512)(128)(4,1)S(1)} %get-tuple-element.273, bf16[2,32,128,128]{3,2,1,0:T(8,128)(2,1)} %get-tuple-element.310, s32[]{:T(128)S(6)} %select_n.94), kind=kOutput, calls=%fused_computation.6.clone.1 | convolution fusion | flops 269484032 | bytes 5242916 | tf_op jit(solution)/shard_map/while/body/eval_jaxpr/sij,sjf->sif/dot_general | solution.py:43
  37.6 0.7 add_compare_fusion.4
  38.3 1.4 fusion.71
  39.7 0.9 copy.10
  40.7 22.0 %reduce-scatter.3.cloned.1.call-done = f32[128,256]{1,0:T(8,128)} async-done(((f32[512,256]{1,0:T(8,128)}), f32[128,256]{1,0:T(8,128)}) %reduce-scatter.3.cloned.1.call-update) | async-done | bytes 131088 | tf_op jit(solution)/shard_map/reduce_scatter | solution.py:66
  62.7 0.9 convert_element_type.15
  63.7 1.3 collective-permute-start
  65.2 1.6 collective-permute-done
  67.0 8.9 %all_gather.7 = bf16[512,256]{1,0:T(8,128)(2,1)S(1)} all-gather(bf16[128,256]{1,0:T(8,128)(2,1)S(1)} %convolution_convert_fusion), channel_id=1, replica_groups=mesh['section'=2,'row'=4,'col'=4] {'row'}, dimensions={0}, use_global_device_ids=true | all-gather | bytes 327680 | tf_op jit(solution)/shard_map/all_gather | solution.py:35
  75.9 0.9 fusion.40
  77.0 19.5 %while.23 = (s32[]{:T(128)}, f32[4,128,256]{2,0,1:T(4,128)S(1)}, s32[2]{0:T(128)S(1)}, s32[2,32,2]{1,2,0:T(2,128)S(1)}, s32[]{:T(128)}, /*index=5*/bf16[2,32,128...) while((s32[]{:T(128)}, f32[4,128,256]{2,0,1:T(4,128)S(1)}, ...), condition=%wide.region_5.7_spmd.clone, body=%wide.region_4.6_spmd.clone.sunk | while | flops 278136320 | bytes 12588737 | solution.py:60
  79.3 2.0 gather_fusion.1
  81.3 2.7 %fusion.76 = bf16[32,128,256]{2,1,0:T(8,128)(2,1)S(1)} fusion(bf16[32,128,256]{2,1,0:T(8,128)(2,1)} %gather_fusion.1, pred[32]{0:T(512)(128)(4,1)S(1)} %get-tuple-element.282, bf16[2,32,128,128]{3,2,1,0:T(8,128)(2,1)} %get-tuple-element.343, s32[]{:T(128)S(6)} %select_n.96), kind=kOutput, calls=%fused_computation.28.clone.1 | convolution fusion | flops 269484032 | bytes 5242916 | tf_op jit(solution)/shard_map/while/body/eval_jaxpr/sij,sjf->sif/dot_general | solution.py:43
  85.2 1.4 fusion.77
  89.0 2.0 gather_fusion.1
  91.0 2.7 %fusion.76 = bf16[32,128,256]{2,1,0:T(8,128)(2,1)S(1)} fusion(bf16[32,128,256]{2,1,0:T(8,128)(2,1)} %gather_fusion.1, pred[32]{0:T(512)(128)(4,1)S(1)} %get-tuple-element.282, bf16[2,32,128,128]{3,2,1,0:T(8,128)(2,1)} %get-tuple-element.343, s32[]{:T(128)S(6)} %select_n.96), kind=kOutput, calls=%fused_computation.28.clone.1 | convolution fusion | flops 269484032 | bytes 5242916 | tf_op jit(solution)/shard_map/while/body/eval_jaxpr/sij,sjf->sif/dot_general | solution.py:43
  95.0 1.4 fusion.77
  96.4 0.9 copy.12
  97.3 83.9 %all-reduce.2.cloned.1.call-done = f32[256,256]{0,1:T(8,128)} async-done(((f32[256,256]{0,1:T(8,128)}), f32[256,256]{0,1:T(8,128)}) %all-reduce.2.cloned.1.call-update) | async-done | bytes 262160 | tf_op jit(solution)/shard_map/psum | solution.py:91
  181.2 1.0 multiply_bitcast_fusion
  182.2 0.8 copy.13
  183.0 21.3 %reduce-scatter.5.cloned.1.call-done = f32[128,256]{1,0:T(8,128)} async-done(((f32[512,256]{1,0:T(8,128)}), f32[128,256]{1,0:T(8,128)}) %reduce-scatter.5.cloned.1.call-update) | async-done | bytes 131088 | tf_op jit(solution)/shard_map/reduce_scatter | solution.py:66
  204.3 1.5 select_bitcast_fusion
  (44 shorter events, 4.6 us)
Async XLA Ops:
  7.2 0.9 copy-start
  7.2 55.6 %reduce-scatter.3.cloned.1.call-start = ((), (), s32[]{:S(2)}) async-start(), calls=%async_computation.2 | async-start | bytes 655360 | tf_op jit(solution)/shard_map/reduce_scatter | solution.py:66
  19.6 45.4 %copy-start.2 = (bf16[1,128,256]{2,1,0:T(8,128)(2,1)S(1)}, bf16[1,128,256]{2,1,0:T(8,128)(2,1)}, u32[]{:S(2)}) copy-start(bf16[1,128,256]{2,1,0:T(8,128)(2,1)} %param.15) | copy-start | bytes 196612
  19.6 45.4 %copy-start.3 = (bf16[128,256]{1,0:T(8,128)(2,1)S(1)}, bf16[128,256]{1,0:T(8,128)(2,1)}, u32[]{:S(2)}) copy-start(bf16[128,256]{1,0:T(8,128)(2,1)} %param.13) | copy-start | bytes 196612
  40.7 140.5 %all-reduce.2.cloned.1.call-start = ((), (), s32[]{:S(2)}) async-start(), calls=%async_computation.3 | async-start | bytes 524288 | tf_op jit(solution)/shard_map/psum | solution.py:91
  63.7 3.1 %collective-permute-start = (bf16[128,256]{1,0:T(8,128)(2,1)S(1)}, bf16[128,256]{1,0:T(8,128)(2,1)S(1)}, u32[]{:S(2)}, u32[]{:S(2)}) collective-permute-start(bf16[128,256]{1,0:T(8,128)(2,1)S(1)} %convert_element_type.15), channel_id=1, source_target_pairs={{16,0},{17,1},{18,2},{19,3},{20,4},{21,5},{22,6},{23,7},{24,8},{25... | collective-permute-start | bytes 196616 | tf_op jit(solution)/shard_map/ppermute | solution.py:11
  76.9 127.4 %reduce-scatter.5.cloned.1.call-start = ((), (), s32[]{:S(2)}) async-start(), calls=%async_computation.4 | async-start | bytes 655360 | tf_op jit(solution)/shard_map/reduce_scatter | solution.py:66
  96.4 107.9 %copy-start.1 = (f32[128,256]{1,0:T(8,128)S(1)}, f32[128,256]{1,0:T(8,128)}, u32[]{:S(2)}) copy-start(f32[128,256]{1,0:T(8,128)} %reduce-scatter.3.cloned.1.call-done) | copy-start | bytes 393220
Sparse Core Ops, SparseCore 0:
  40.8 21.9 reduce-scatter.2
  77.0 104.1 all-reduce.1
  183.6 20.6 reduce-scatter.4
where the time goes:
time: 213 us; the launch traced here: 212 us
  waiting for transfers between devices  129 us (61%)
  blocking collectives  19.4 us (9%)
  matrix products  18.1 us (8%)
  local copies, waits for them, and re-layouts  13.9 us (7%)
  between operations  13.9 us (7%)
  loops' own time  9.92 us (5%)
  other arithmetic  6.98 us (3%)
    psum x1, waiting for transfers between devices, on_device(): total_weight = lax.psum(local_weight, ('row', 'col'))  83.9 us
    reduce_scatter x2, waiting for transfers between devices, reduce_col(): lax.psum_scatter(block_total(source, col_blocks), 'col', scatter_dimensio...  43.3 us
    all_gather x2, blocking collectives, spread(): return lax.all_gather(row_grad, 'row', axis=0, tiled=True)  19.4 us
    dot_general x4, matrix products, group_term(): jnp.einsum('sij,sjf->sif', blocks_here, picked, preferred_element_type=jn...  10.8 us
    another operation x2, loops' own time, block_total(): lax.scan(scan_step, start_total, jnp.arange(groups, dtype=jnp.int32))  9.92 us
    gather x4, local copies, waits for them, and re-layouts, group_term(): picked = jnp.take(col_blocks, slots_here[:, 1], axis=0)  8.08 us
    dot_general x4, matrix products, group_term(): return total + jnp.einsum('bs,sif->bif', select, products)  5.75 us
  transfers between devices with their start and end apart: 4, of which 4 were waited for; matrix products, arithmetic and copies ran while one was open for 8% of the time, Pallas kernels for 0%

commit v1 on v0

--- a/solution.py
+++ b/solution.py
@@ -3,6 +3,7 @@
 import jax.numpy as jnp
 from jax import lax
 from jax.sharding import PartitionSpec as P
+from jax.lax import psum
 
 
 def from_behind(value, axis, steps):
@@ -88,7 +89,8 @@
     second_weight, second_grad = backward_step(received)
     local_weight = jnp.where(upper, first_weight, second_weight)
     feature_block = jnp.where(upper, first_grad, second_grad)
-    total_weight = lax.psum(local_weight, ("row", "col"))
+    y_new = psum(local_weight, axis_name="col")
+    total_weight = psum(y_new, axis_name="row")
     node_total = node_rows * lax.axis_size("row") * lax.axis_size("col")
     weight_grad = (total_weight * (1.0 / math.sqrt(node_total)))[None]
     return (weight_grad, feature_block[None])

time: 213 us -> 180 us (0.85)
  waiting for transfers between devices: 129 us -> 95 us
    psum x1 -> x2, waiting for transfers between devices: 83.9 us -> 49.4 us  [the longest x1 24.8 us: on_device(): total_weight = psum(y_new, axis_name='row')]
  transfers between devices with their start and end apart: 4 -> 5, of which waited for: 4 -> 5; matrix products, arithmetic and copies ran while one was open for 8% -> 10% of each run, Pallas kernels for 0% -> 0%
where the time goes in v1:
time: 180 us; the launch traced here: 179 us
  waiting for transfers between devices  95 us (53%)
  blocking collectives  19.4 us (11%)
  matrix products  18 us (10%)
  local copies, waits for them, and re-layouts  13.9 us (8%)
  between operations  13.9 us (8%)
  loops' own time  10.6 us (6%)
  other arithmetic  6.98 us (4%)
    reduce_scatter x2, waiting for transfers between devices, reduce_col(): lax.psum_scatter(block_total(source, col_blocks), 'col', scatter_dimensio...  44 us
    psum x1, waiting for transfers between devices, on_device(): total_weight = psum(y_new, axis_name='row')  24.8 us
    psum x1, waiting for transfers between devices, on_device(): y_new = psum(local_weight, axis_name='col')  24.6 us
    all_gather x2, blocking collectives, spread(): return lax.all_gather(row_grad, 'row', axis=0, tiled=True)  19.4 us
    dot_general x4, matrix products, group_term(): jnp.einsum('sij,sjf->sif', blocks_here, picked, preferred_element_type=jn...  10.8 us
    another operation x2, loops' own time, block_total(): lax.scan(scan_step, start_total, jnp.arange(groups, dtype=jnp.int32))  10.6 us
    gather x4, local copies, waits for them, and re-layouts, group_term(): picked = jnp.take(col_blocks, slots_here[:, 1], axis=0)  8.08 us
    dot_general x4, matrix products, group_term(): return total + jnp.einsum('bs,sif->bif', select, products)  5.75 us
  transfers between devices with their start and end apart: 5, of which 5 were waited for; matrix products, arithmetic and copies ran while one was open for 10% of the time, Pallas kernels for 0%

profile of v1, /device:TPU:0, one launch (start us, length us, event | category | flops | bytes accessed | tf_op | source)
XLA Modules:
  0.0 179.3 jit_solution(14495105843355704719)
XLA Ops:
  7.2 0.9 broadcast_compare_fusion
  8.3 10.5 %all_gather.6 = bf16[512,256]{1,0:T(8,128)(2,1)S(1)} all-gather(bf16[128,256]{1,0:T(8,128)(2,1)S(1)} %convolution_convert_fusion.1), channel_id=1, replica_groups=mesh['section'=2,'row'=4,'col'=4] {'row'}, dimensions={0}, use_global_device_ids=true | all-gather | bytes 327680 | tf_op jit(solution)/shard_map/all_gather | solution.py:36
  18.8 0.8 reshape_squeeze.7
  19.6 20.1 %while.22 = (s32[]{:T(128)}, f32[4,128,256]{2,0,1:T(4,128)S(1)}, s32[2]{0:T(128)S(1)}, s32[2,32,2]{1,2,0:T(2,128)S(1)}, s32[]{:T(128)}, /*index=5*/bf16[2,32,128...) while((s32[]{:T(128)}, f32[4,128,256]{2,0,1:T(4,128)S(1)}, ...), condition=%wide.region_1.3_spmd.clone, body=%wide.region_0.2_spmd.clone.sunk | while | flops 278136320 | bytes 12588737 | solution.py:61
  22.2 2.0 %gather_fusion = bf16[32,128,256]{2,1,0:T(8,128)(2,1)} fusion(bf16[4,128,256]{2,1,0:T(8,128)(2,1)S(1)} %get-tuple-element.311, s32[1024]{0:T(1024)S(1)} %pad_clamp_fusion.4), kind=kCustom, calls=%fused_computation.clone.clone.1 | custom fusion | bytes 4194432 | tf_op jit(solution)/shard_map/while/body/eval_jaxpr/jit(_take)/gather | solution.py:43
  24.2 2.7 %fusion.70 = bf16[32,128,256]{2,1,0:T(8,128)(2,1)S(1)} fusion(bf16[32,128,256]{2,1,0:T(8,128)(2,1)} %gather_fusion, pred[32]{0:T(512)(128)(4,1)S(1)} %get-tuple-element.273, bf16[2,32,128,128]{3,2,1,0:T(8,128)(2,1)} %get-tuple-element.310, s32[]{:T(128)S(6)} %select_n.94), kind=kOutput, calls=%fused_computation.6.clone.1 | convolution fusion | flops 269484032 | bytes 5242916 | tf_op jit(solution)/shard_map/while/body/eval_jaxpr/sij,sjf->sif/dot_general | solution.py:44
  28.2 1.4 fusion.71
  32.3 2.0 %gather_fusion = bf16[32,128,256]{2,1,0:T(8,128)(2,1)} fusion(bf16[4,128,256]{2,1,0:T(8,128)(2,1)S(1)} %get-tuple-element.311, s32[1024]{0:T(1024)S(1)} %pad_clamp_fusion.4), kind=kCustom, calls=%fused_computation.clone.clone.1 | custom fusion | bytes 4194432 | tf_op jit(solution)/shard_map/while/body/eval_jaxpr/jit(_take)/gather | solution.py:43
  34.3 2.7 %fusion.70 = bf16[32,128,256]{2,1,0:T(8,128)(2,1)S(1)} fusion(bf16[32,128,256]{2,1,0:T(8,128)(2,1)} %gather_fusion, pred[32]{0:T(512)(128)(4,1)S(1)} %get-tuple-element.273, bf16[2,32,128,128]{3,2,1,0:T(8,128)(2,1)} %get-tuple-element.310, s32[]{:T(128)S(6)} %select_n.94), kind=kOutput, calls=%fused_computation.6.clone.1 | convolution fusion | flops 269484032 | bytes 5242916 | tf_op jit(solution)/shard_map/while/body/eval_jaxpr/sij,sjf->sif/dot_general | solution.py:44
  38.3 1.4 fusion.71
  39.7 0.9 copy.10
  40.7 22.0 %reduce-scatter.3.cloned.1.call-done = f32[128,256]{1,0:T(8,128)} async-done(((f32[512,256]{1,0:T(8,128)}), f32[128,256]{1,0:T(8,128)}) %reduce-scatter.3.cloned.1.call-update) | async-done | bytes 131088 | tf_op jit(solution)/shard_map/reduce_scatter | solution.py:67
  62.7 0.9 convert_element_type.15
  63.7 1.3 collective-permute-start
  65.2 1.6 collective-permute-done
  66.8 0.9 fusion.40
  68.0 8.9 %all_gather.7 = bf16[512,256]{1,0:T(8,128)(2,1)S(1)} all-gather(bf16[128,256]{1,0:T(8,128)(2,1)S(1)} %convolution_convert_fusion), channel_id=1, replica_groups=mesh['section'=2,'row'=4,'col'=4] {'row'}, dimensions={0}, use_global_device_ids=true | all-gather | bytes 327680 | tf_op jit(solution)/shard_map/all_gather | solution.py:36
  76.9 24.6 %all-reduce.3.cloned.1.call-done = f32[256,256]{0,1:T(8,128)} async-done(((f32[256,256]{0,1:T(8,128)}), f32[256,256]{0,1:T(8,128)}) %all-reduce.3.cloned.1.call-update) | async-done | bytes 262160 | tf_op jit(solution)/shard_map/psum | solution.py:92
  101.6 20.1 %while.23 = (s32[]{:T(128)}, f32[4,128,256]{2,0,1:T(4,128)S(1)}, s32[2]{0:T(128)S(1)}, s32[2,32,2]{1,2,0:T(2,128)S(1)}, s32[]{:T(128)}, /*index=5*/bf16[2,32,128...) while((s32[]{:T(128)}, f32[4,128,256]{2,0,1:T(4,128)S(1)}, ...), condition=%wide.region_6.8_spmd.clone, body=%wide.region_5.7_spmd.clone.sunk | while | flops 278136320 | bytes 12588737 | solution.py:61
  104.2 2.0 %gather_fusion.1 = bf16[32,128,256]{2,1,0:T(8,128)(2,1)} fusion(bf16[4,128,256]{2,1,0:T(8,128)(2,1)S(1)} %get-tuple-element.344, s32[1024]{0:T(1024)S(1)} %pad_clamp_fusion.5), kind=kCustom, calls=%fused_computation.1.clone.clone.1 | custom fusion | bytes 4194432 | tf_op jit(solution)/shard_map/while/body/eval_jaxpr/jit(_take)/gather | solution.py:43
  106.2 2.7 %fusion.76 = bf16[32,128,256]{2,1,0:T(8,128)(2,1)S(1)} fusion(bf16[32,128,256]{2,1,0:T(8,128)(2,1)} %gather_fusion.1, pred[32]{0:T(512)(128)(4,1)S(1)} %get-tuple-element.282, bf16[2,32,128,128]{3,2,1,0:T(8,128)(2,1)} %get-tuple-element.343, s32[]{:T(128)S(6)} %select_n.96), kind=kOutput, calls=%fused_computation.28.clone.1 | convolution fusion | flops 269484032 | bytes 5242916 | tf_op jit(solution)/shard_map/while/body/eval_jaxpr/sij,sjf->sif/dot_general | solution.py:44
  109.6 0.7 add_compare_fusion.5
  110.3 1.4 fusion.77
  114.3 2.0 %gather_fusion.1 = bf16[32,128,256]{2,1,0:T(8,128)(2,1)} fusion(bf16[4,128,256]{2,1,0:T(8,128)(2,1)S(1)} %get-tuple-element.344, s32[1024]{0:T(1024)S(1)} %pad_clamp_fusion.5), kind=kCustom, calls=%fused_computation.1.clone.clone.1 | custom fusion | bytes 4194432 | tf_op jit(solution)/shard_map/while/body/eval_jaxpr/jit(_take)/gather | solution.py:43
  116.3 2.7 %fusion.76 = bf16[32,128,256]{2,1,0:T(8,128)(2,1)S(1)} fusion(bf16[32,128,256]{2,1,0:T(8,128)(2,1)} %gather_fusion.1, pred[32]{0:T(512)(128)(4,1)S(1)} %get-tuple-element.282, bf16[2,32,128,128]{3,2,1,0:T(8,128)(2,1)} %get-tuple-element.343, s32[]{:T(128)S(6)} %select_n.96), kind=kOutput, calls=%fused_computation.28.clone.1 | convolution fusion | flops 269484032 | bytes 5242916 | tf_op jit(solution)/shard_map/while/body/eval_jaxpr/sij,sjf->sif/dot_general | solution.py:44
  120.3 1.4 fusion.77
  121.8 0.9 copy.12
  122.7 24.8 %all-reduce.5.cloned.1.call-done = f32[256,256]{0,1:T(8,128)} async-done(((f32[256,256]{0,1:T(8,128)}), f32[256,256]{0,1:T(8,128)}) %all-reduce.5.cloned.1.call-update) | async-done | bytes 262160 | tf_op jit(solution)/shard_map/psum | solution.py:93
  147.5 1.0 multiply_bitcast_fusion
  148.4 0.8 copy.13
  149.3 22.0 %reduce-scatter.5.cloned.1.call-done = f32[128,256]{1,0:T(8,128)} async-done(((f32[512,256]{1,0:T(8,128)}), f32[128,256]{1,0:T(8,128)}) %reduce-scatter.5.cloned.1.call-update) | async-done | bytes 131088 | tf_op jit(solution)/shard_map/reduce_scatter | solution.py:67
  171.2 1.5 select_bitcast_fusion
  (47 shorter events, 5.3 us)
Async XLA Ops:
  7.2 0.9 copy-start
  7.2 55.6 %reduce-scatter.3.cloned.1.call-start = ((), (), s32[]{:S(2)}) async-start(), calls=%async_computation.2 | async-start | bytes 655360 | tf_op jit(solution)/shard_map/reduce_scatter | solution.py:67
  19.6 45.4 %copy-start.2 = (bf16[1,128,256]{2,1,0:T(8,128)(2,1)S(1)}, bf16[1,128,256]{2,1,0:T(8,128)(2,1)}, u32[]{:S(2)}) copy-start(bf16[1,128,256]{2,1,0:T(8,128)(2,1)} %param.15) | copy-start | bytes 196612
  19.6 45.4 %copy-start.3 = (bf16[128,256]{1,0:T(8,128)(2,1)S(1)}, bf16[128,256]{1,0:T(8,128)(2,1)}, u32[]{:S(2)}) copy-start(bf16[128,256]{1,0:T(8,128)(2,1)} %param.13) | copy-start | bytes 196612
  40.7 60.9 %all-reduce.3.cloned.1.call-start = ((), (), s32[]{:S(2)}) async-start(), calls=%async_computation.3 | async-start | bytes 524288 | tf_op jit(solution)/shard_map/psum | solution.py:92
  63.7 3.1 %collective-permute-start = (bf16[128,256]{1,0:T(8,128)(2,1)S(1)}, bf16[128,256]{1,0:T(8,128)(2,1)S(1)}, u32[]{:S(2)}, u32[]{:S(2)}) collective-permute-start(bf16[128,256]{1,0:T(8,128)(2,1)S(1)} %convert_element_type.15), channel_id=1, source_target_pairs={{16,0},{17,1},{18,2},{19,3},{20,4},{21,5},{22,6},{23,7},{24,8},{25... | collective-permute-start | bytes 196616 | tf_op jit(solution)/shard_map/ppermute | solution.py:12
  67.7 79.7 %all-reduce.5.cloned.1.call-start = ((), (), s32[]{:S(2)}) async-start(), calls=%async_computation.4 | async-start | bytes 524288 | tf_op jit(solution)/shard_map/psum | solution.py:93
  101.6 69.7 %reduce-scatter.5.cloned.1.call-start = ((), (), s32[]{:S(2)}) async-start(), calls=%async_computation.5 | async-start | bytes 655360 | tf_op jit(solution)/shard_map/reduce_scatter | solution.py:67
  121.8 49.5 %copy-start.1 = (f32[128,256]{1,0:T(8,128)S(1)}, f32[128,256]{1,0:T(8,128)}, u32[]{:S(2)}) copy-start(f32[128,256]{1,0:T(8,128)} %reduce-scatter.3.cloned.1.call-done) | copy-start | bytes 393220
Sparse Core Ops, SparseCore 0:
  40.8 21.9 reduce-scatter.2
  67.9 33.6 all-reduce.2
  104.7 42.6 all-reduce.4
  149.6 21.6 reduce-scatter.4
